TPU v7x, 256 devices: a whole 4x4x8 slice. The times are simulated.
256 devices in a mesh: grp: 8 (over z), ep: 32 (over y, x, core).
Axes of the slice: x: 4, y: 4, z: 8, core: 2. Of those that a mesh axis runs over, the one named last changes fastest.
Arguments:
- pol_hidden: bfloat16 [10240, 1024], P(('grp', 'ep')), may hold values from -80 to 80
- ref_hidden: bfloat16 [10240, 1024], P(('grp', 'ep')), may hold values from -80 to 80
- pol_routes: int32 [10240, 8], P(('grp', 'ep')), may hold values from 0 to 63, all different within a row; in each aligned block of 40 rows (0 to 39, 40 to 79, ...) at most 7 rows name the same one
- ref_routes: int32 [10240, 8], P(('grp', 'ep')), may hold values from 0 to 63, all different within a row; in each aligned block of 40 rows (0 to 39, 40 to 79, ...) at most 7 rows name the same one
- pol_gates: float32 [10240, 8], P(('grp', 'ep')), may hold values from 0.02 to 0.3
- ref_gates: float32 [10240, 8], P(('grp', 'ep')), may hold values from 0.02 to 0.3
- w_gate: bfloat16 [64, 1024, 384], P('ep'), may hold values from -0.1875 to 0.1875
- w_up: bfloat16 [64, 1024, 384], P('ep'), may hold values from -0.1875 to 0.1875
- w_down: bfloat16 [64, 384, 1024], P('ep'), may hold values from -0.3125 to 0.3125
- norm_gain: float32 [1024], replicated, may hold values from 0.5 to 1.5
- vocab_head: bfloat16 [77824, 1024], P(('grp', 'ep')), may hold values from -2 to 2
- targets: int32 [10240], P(('grp', 'ep')), may hold values from 0 to 77823
- seq_lengths: int32 [256], replicated, may hold values from 1 to 1024, 10240 in all
- owners: int32 [256], replicated, may hold values from 0 to 255, each once
Outputs:
- token_ratio: float32 [10240], P(('grp', 'ep'))
- owned_mean: float32 [256], P(('grp', 'ep'))
Inputs may be any that keep to these rules, and one draw needn't show every extreme that they name: `pol_routes`: each row names 8 different experts; among the 40 rows of one device no expert is named by more than 7 rows, a bound that some block reaches. `ref_routes`: each row names 8 different experts; among the 40 rows of one device no expert is named by more than 7 rows, a bound that some block reaches. `seq_lengths`: the lengths sum to 10240; the longest is exactly 1024. `owners`: every device index appears exactly once.
All inputs are finite; a program needn't handle non-finite values.
Results may differ from a plain program's by a relative error of at most 0.0062.
Values may be sent and summed in bfloat16 or wider, within the bound.
A program may use at most 128 MiB of HBM per device.

v0:
```python
import jax
import jax.numpy as jnp
from jax import lax
from jax.sharding import PartitionSpec as P


def joined_2(value, axis, join):
    pieces = jax.tree.map(lambda part: lax.all_gather(part, axis), value)
    head = jax.tree.map(lambda part: part[0], pieces)
    tail = jax.tree.map(lambda part: part[1:], pieces)
    so_far, _ = lax.scan(lambda so_far, share: (join(so_far, share), None), head, tail)
    return so_far


def combine_stats(earlier_part, second):
    peak = jnp.maximum(earlier_part[0], second[0])
    totals = earlier_part[1] * jnp.exp(earlier_part[0] - peak) + second[1] * jnp.exp(
        second[0] - peak
    )
    return (peak, totals, earlier_part[2] + second[2])


def vocab_stats(row_block, weights, vocab_ids, wanted):
    logits = jnp.einsum("td,vd->tv", row_block, weights, preferred_element_type=jnp.float32)
    peak = jnp.max(logits, axis=1)
    totals = jnp.sum(jnp.exp(logits - peak[:, None]), axis=1)
    picked = jnp.sum(jnp.where(vocab_ids[None, :] == wanted[:, None], logits, 0.0), axis=1)
    return (peak, totals, picked)


def expert_tables(routes, gates, experts, capacity):
    route_hits = routes[:, :, None] == jnp.arange(experts, dtype=jnp.int32)[None, None, :]
    members = jnp.sum(route_hits.astype(jnp.int32), axis=1)
    earlier = jnp.cumsum(members, axis=0) - members
    placed = (members[:, :, None] > 0) & (
        earlier[:, :, None] == jnp.arange(capacity, dtype=jnp.int32)[None, None, :]
    )
    weight = jnp.sum(jnp.where(route_hits, gates[:, :, None], 0.0), axis=1)
    tok_count = routes.shape[0]
    picker = placed.astype(jnp.bfloat16).reshape(tok_count, experts * capacity)
    mixing = (weight[:, :, None] * placed.astype(jnp.float32)).reshape(
        tok_count, experts * capacity
    )
    return (picker, mixing)


def local(
    pol_hidden,
    ref_hidden,
    pol_routes,
    ref_routes,
    pol_gates,
    ref_gates,
    w_gate,
    w_up,
    w_down,
    norm_gain,
    vocab_head,
    targets,
    seq_lengths,
    owners,
):
    groups = lax.axis_size("ep")
    device_index = lax.axis_index(("grp", "ep"))
    local_experts = w_gate.shape[0]
    experts = local_experts * groups
    tok_count = pol_hidden.shape[0]
    width = pol_hidden.shape[1]
    fanout = pol_routes.shape[1]
    capacity = tok_count * fanout // experts + 2
    pol_pick, pol_mixing = expert_tables(pol_routes, pol_gates, experts, capacity)
    ref_pick, ref_mixing = expert_tables(ref_routes, ref_gates, experts, capacity)
    pol_send = jnp.einsum(
        "ts,td->sd", pol_pick, pol_hidden, preferred_element_type=jnp.float32
    ).astype(jnp.bfloat16)
    ref_send = jnp.einsum(
        "ts,td->sd", ref_pick, ref_hidden, preferred_element_type=jnp.float32
    ).astype(jnp.bfloat16)
    pol_send = pol_send.reshape(groups, local_experts, capacity, width)
    ref_send = ref_send.reshape(groups, local_experts, capacity, width)
    pol_part = lax.all_to_all(pol_send, "ep", split_axis=0, concat_axis=0, tiled=True)
    ref_part = lax.all_to_all(ref_send, "ep", split_axis=0, concat_axis=0, tiled=True)
    slots = pol_part.shape[2]
    joined = jnp.concatenate((pol_part, ref_part), axis=2)
    gate_act = jnp.einsum("nesd,edf->nesf", joined, w_gate, preferred_element_type=jnp.float32)
    up_act = jnp.einsum("nesd,edf->nesf", joined, w_up, preferred_element_type=jnp.float32)
    inner = (jax.nn.silu(gate_act) * up_act).astype(jnp.bfloat16)
    outputs = jnp.einsum(
        "nesf,efd->nesd", inner, w_down, preferred_element_type=jnp.float32
    ).astype(jnp.bfloat16)
    pol_back = lax.all_to_all(outputs[:, :, :slots], "ep", split_axis=0, concat_axis=0, tiled=True)
    ref_back = lax.all_to_all(outputs[:, :, slots:], "ep", split_axis=0, concat_axis=0, tiled=True)

    def mix_back(hidden, mixing, back):
        rows_back = back.reshape(experts * capacity, width).astype(jnp.float32)
        mixed = hidden.astype(jnp.float32) + jnp.dot(
            mixing, rows_back, precision=lax.Precision.HIGHEST
        )
        scale = lax.rsqrt(jnp.mean(mixed * mixed, axis=1, keepdims=True) + 1e-06)
        return (mixed * scale * norm_gain).astype(jnp.bfloat16)

    pol_normed = mix_back(pol_hidden, pol_mixing, pol_back)
    ref_normed = mix_back(ref_hidden, ref_mixing, ref_back)
    vocab_rows = vocab_head.shape[0]
    band = lax.axis_index("grp")
    pol_col, ref_col, wanted = (
        lax.all_gather(pol_normed, "grp", axis=0, tiled=True),
        lax.all_gather(ref_normed, "grp", axis=0, tiled=True),
        lax.all_gather(targets, "grp", axis=0, tiled=True),
    )
    col_count = wanted.shape[0]
    floor_value = jnp.full((2, col_count), -1e30, jnp.float32)
    blank = jnp.zeros((2, col_count), jnp.float32)
    piece = lax.all_gather(vocab_head, "ep", axis=0, tiled=True)
    count = piece.shape[0]
    place = jnp.arange(count, dtype=jnp.int32)
    vocab_ids = band * groups * vocab_rows + place
    pol_stats = vocab_stats(pol_col, piece, vocab_ids, wanted)
    ref_stats = vocab_stats(ref_col, piece, vocab_ids, wanted)
    fresh = tuple(
        (jnp.stack((pol_part, ref_part)) for pol_part, ref_part in zip(pol_stats, ref_stats))
    )
    stats = combine_stats((floor_value, blank, blank), fresh)
    peak, totals, picked = joined_2(stats, "grp", combine_stats)
    logprob = picked - (peak + jnp.log(totals))
    mine = lax.dynamic_slice_in_dim(logprob, band * tok_count, tok_count, axis=1)
    token_ratio = mine[0] - mine[1]
    offsets = jnp.cumsum(seq_lengths) - seq_lengths
    positions = device_index * tok_count + jnp.arange(tok_count, dtype=jnp.int32)
    inside = (positions[:, None] >= offsets[None, :]) & (
        positions[:, None] < (offsets + seq_lengths)[None, :]
    )
    partial_value = jnp.dot(
        token_ratio, inside.astype(jnp.float32), precision=lax.Precision.HIGHEST
    ) / seq_lengths.astype(jnp.float32)
    sums = lax.psum(partial_value, ("grp", "ep"))
    owned = jnp.sum(jnp.where(owners == device_index, sums, 0.0)).reshape(1)
    return (token_ratio, owned)


def solution(mesh):
    return jax.shard_map(
        local,
        mesh=mesh,
        in_specs=(
            P(("grp", "ep"), None),
            P(("grp", "ep"), None),
            P(("grp", "ep"), None),
            P(("grp", "ep"), None),
            P(("grp", "ep"), None),
            P(("grp", "ep"), None),
            P("ep", None, None),
            P("ep", None, None),
            P("ep", None, None),
            P(),
            P(("grp", "ep"), None),
            P(("grp", "ep")),
            P(),
            P(),
        ),
        out_specs=(P(("grp", "ep")), P(("grp", "ep"))),
        check_vma=False,
    )
```

profile of v0, /device:TPU:1, one launch (start us, length us, event | category | flops | bytes accessed | tf_op | source)
XLA Modules:
  0.0 389.7 jit_solution(15554492775969641314)
XLA Ops:
  7.2 0.7 all-gather.4.cloned.1.call-update
  7.9 0.8 copy.62
  8.9 0.4 copy-done.13
  9.4 0.6 copy-done.9
  10.4 0.6 copy-done.18
  11.0 0.4 convolution_convert_fusion.1
  11.8 2.0 copy.67
  13.7 8.7 %all-to-all-start = ((bf16[32,2,7,1024]{3,1,2,0:T(2,128)(2,1)}), bf16[32,2,7,1024]{3,1,2,0:T(2,128)(2,1)S(1)}, u32[]{:S(2)}, u32[]{:S(2)}) async-start(bf16[32,2,7,1024]{3,1,2,0:T(2,128)(2,1)} %copy.67), calls=%async_computation | async-start | bytes 1835008 | tf_op jit(solution)/shard_map/all_to_all | solution.py:81
  22.7 0.4 copy-done.15
  23.2 0.6 copy-done.11
  24.1 1.4 convolution_convert_fusion
  25.5 1.4 reshape.318
  27.0 2.0 copy.71
  28.9 12.9 %all-to-all-done = bf16[32,2,7,1024]{3,1,2,0:T(2,128)(2,1)S(1)} async-done(((bf16[32,2,7,1024]{3,1,2,0:T(2,128)(2,1)}), bf16[32,2,7,1024]{3,1,2,0:T(2,128)(2,1)S(1)}, u32[]{:S(2)}, u32[]{:S(2)}) %all-to-all-start) | async-done | bytes 917536 | tf_op jit(solution)/shard_map/all_to_all | solution.py:81
  41.8 0.9 copy-done.2
  42.7 5.4 %all-to-all-start.1 = ((bf16[32,2,7,1024]{3,1,2,0:T(2,128)(2,1)}), bf16[32,2,7,1024]{3,1,2,0:T(2,128)(2,1)}, u32[]{:S(2)}, u32[]{:S(2)}) async-start(bf16[32,2,7,1024]{3,1,2,0:T(2,128)(2,1)} %copy.71), calls=%async_computation.1 | async-start | bytes 1835008 | tf_op jit(solution)/shard_map/all_to_all | solution.py:82
  48.2 1.4 copy_dynamic-update-slice_fusion.1
  49.6 14.5 %all-to-all-done.1 = bf16[32,2,7,1024]{3,1,2,0:T(2,128)(2,1)} async-done(((bf16[32,2,7,1024]{3,1,2,0:T(2,128)(2,1)}), bf16[32,2,7,1024]{3,1,2,0:T(2,128)(2,1)}, u32[]{:S(2)}, u32[]{:S(2)}) %all-to-all-start.1) | async-done | bytes 917536 | tf_op jit(solution)/shard_map/all_to_all | solution.py:82
  64.1 1.5 copy_dynamic-update-slice_fusion
  65.8 2.2 fusion.9
  68.0 5.2 %convert_bitcast_fusion = bf16[32,2,14,1024]{3,0,2,1:T(8,128)(2,1)} fusion(bf16[2,384,1024]{2,1,0:T(8,128)(2,1)S(1)} %copy-done, bf16[32,2,14,1024]{3,0,2,1:T(8,128)(2,1)S(1)} %copy_dynamic-update-slice_fusion, bf16[2,1024,384]{2,1,0:T(8,128)(2,1)} %param.23, f32[32,2,14,384]{3,0,2,1:T(8,128)} %fusion.9), kind=kOutput, calls=%fused_computation.12 | convolution fusion | flops 1412268032 | bytes 8192000 | tf_op jit(solution)/shard_map/nesf,efd->nesd/dot_general | solution.py:88
  73.2 1.9 fusion.44
  75.2 1.9 copy.78
  77.1 3.9 all-to-all-start.3
  81.8 1.9 copy.74
  83.7 21.1 %all-to-all-done.3 = bf16[32,2,7,1024]{3,1,2,0:T(2,128)(2,1)S(1)} async-done(((bf16[32,2,7,1024]{3,1,2,0:T(2,128)(2,1)}), bf16[32,2,7,1024]{3,1,2,0:T(2,128)(2,1)S(1)}, u32[]{:S(2)}, u32[]{:S(2)}) %all-to-all-start.3) | async-done | bytes 917536 | tf_op jit(solution)/shard_map/all_to_all | solution.py:92
  104.8 6.1 %all-to-all-start.2 = ((bf16[32,2,7,1024]{3,1,2,0:T(2,128)(2,1)}), bf16[32,2,7,1024]{3,1,2,0:T(2,128)(2,1)S(1)}, u32[]{:S(2)}, u32[]{:S(2)}) async-start(bf16[32,2,7,1024]{3,1,2,0:T(2,128)(2,1)} %copy.74), calls=%async_computation.2 | async-start | bytes 1835008 | tf_op jit(solution)/shard_map/all_to_all | solution.py:91
  111.0 0.7 mul.94
  112.2 0.6 dynamic-slice
  113.7 20.4 %all-reduce = s32[320]{0:T(512)S(1)} all-reduce(s32[320]{0:T(512)S(1)} %dynamic-update-slice), channel_id=1, replica_groups=mesh['grp'=8,'ep'=32] {'grp'}, use_global_device_ids=true, to_apply=%add | all-reduce | flops 320 | bytes 2560
  134.0 0.6 iota_add_fusion.1
  134.7 0.6 fusion.43
  135.4 0.6 iota_add_fusion
  136.3 1.2 reshape.320
  138.1 0.6 copy-done.3
  138.7 0.7 multiply_reduce_fusion
  139.4 1.7 multiply_reduce_fusion.1
  141.2 20.2 %all_gather.26 = bf16[320,1024]{1,0:T(8,128)(2,1)S(1)} all-gather(bf16[40,1024]{1,0:T(8,128)(2,1)S(1)} %get-tuple-element.71), channel_id=1, replica_groups=mesh['grp'=8,'ep'=32] {'grp'}, dimensions={0}, use_global_device_ids=true | all-gather | bytes 737280 | tf_op jit(solution)/shard_map/all_gather | solution.py:107
  161.4 20.5 %all_gather.28 = bf16[320,1024]{1,0:T(8,128)(2,1)S(1)} all-gather(bf16[40,1024]{1,0:T(8,128)(2,1)S(1)} %get-tuple-element.72), channel_id=1, replica_groups=mesh['grp'=8,'ep'=32] {'grp'}, dimensions={0}, use_global_device_ids=true | all-gather | bytes 737280 | tf_op jit(solution)/shard_map/all_gather | solution.py:108
  181.9 13.4 %fusion.45 = (f32[320]{0:T(512)S(1)}, f32[320,9728]{1,0:T(8,128)}) fusion(bf16[320,1024]{1,0:T(8,128)(2,1)S(1)} %all_gather.26, bf16[9728,1024]{1,0:T(8,128)(2,1)} %all-gather.4.cloned.1.call-done), kind=kOutput, calls=%fused_computation.84 | convolution fusion | flops 6378454528 | bytes 33031424 | tf_op jit(solution)/shard_map/td,vd->tv/dot_general | solution.py:24
  195.3 13.5 %fusion.46 = (f32[320]{0:T(512)S(1)}, f32[320,9728]{1,0:T(8,128)}) fusion(bf16[320,1024]{1,0:T(8,128)(2,1)S(1)} %all_gather.28, bf16[9728,1024]{1,0:T(8,128)(2,1)} %all-gather.4.cloned.1.call-done), kind=kOutput, calls=%fused_computation.85 | convolution fusion | flops 6378454528 | bytes 33031424 | tf_op jit(solution)/shard_map/td,vd->tv/dot_general | solution.py:24
  208.8 11.5 %fusion.2 = (f32[320]{0:T(512)S(1)}, f32[320]{0:T(512)S(1)}, f32[320]{0:T(512)S(1)}, f32[320]{0:T(512)S(1)}) fusion(f32[320,9728]{1,0:T(8,128)} %get-tuple-element.80, s32[9728]{0:T(1024)S(1)} %copy-done.17, s32[320]{0:T(512)S(1)} %all-reduce, f32[320]{0:T(512)S(1)} %get-tuple-element.79, f32[320,9728]{1,0:T(8,128)} %get-tuple-element.82, ...), kind=kLoop, calls=%fused_computation.8 | loop fusion | flops 28015360 | bytes 24951552 | tf_op jit(solution)/shard_map/reduce_sum | solution.py:27
  220.3 18.0 %all-gather.1 = f32[8,2,320]{2,1,0:T(2,128)S(1)} all-gather(f32[1,2,320]{2,1,0:T(2,128)S(1)} %maximum_bitcast_fusion), channel_id=2, replica_groups=mesh['grp'=8,'ep'=32] {'grp'}, dimensions={0}, use_global_device_ids=true | all-gather | bytes 23040 | tf_op jit(solution)/shard_map/all_gather | solution.py:8
  238.4 18.0 %all_gather.30 = f32[8,2,320]{2,1,0:T(2,128)S(1)} all-gather(f32[1,2,320]{2,1,0:T(2,128)S(1)} %get-tuple-element.73), channel_id=1, replica_groups=mesh['grp'=8,'ep'=32] {'grp'}, dimensions={0}, use_global_device_ids=true | all-gather | bytes 23040 | tf_op jit(solution)/shard_map/all_gather | solution.py:8
  256.5 18.0 %all_gather.29 = f32[8,2,320]{2,1,0:T(2,128)S(1)} all-gather(f32[1,2,320]{2,1,0:T(2,128)S(1)} %get-tuple-element.74), channel_id=1, replica_groups=mesh['grp'=8,'ep'=32] {'grp'}, dimensions={0}, use_global_device_ids=true | all-gather | bytes 23040 | tf_op jit(solution)/shard_map/all_gather | solution.py:8
  274.9 0.5 fusion.42
  275.7 106.6 %psum.7 = f32[256]{0:T(256)S(1)} all-reduce(f32[256]{0:T(256)S(1)} %convert_divide_fusion), channel_id=1, replica_groups=mesh['grp'=8,'ep'=32] {'grp','ep'}, use_global_device_ids=true, to_apply=%region_18.19 | all-reduce | flops 256 | bytes 2048 | tf_op jit(solution)/shard_map/psum | solution.py:136
  382.2 0.6 fusion.39
  (125 shorter events, 5.3 us)
Async XLA Ops:
  7.2 60.8 %copy-start = (bf16[2,384,1024]{2,1,0:T(8,128)(2,1)S(1)}, bf16[2,384,1024]{2,1,0:T(8,128)(2,1)}, u32[]{:S(2)}) copy-start(bf16[2,384,1024]{2,1,0:T(8,128)(2,1)} %param.24) | copy-start | bytes 4718596
  7.2 3.8 copy-start.7
  7.2 174.7 %all-gather.4.cloned.1.call-start = ((), (), s32[]{:S(2)}) async-start(), calls=%async_computation.4 | async-start | bytes 20545536 | tf_op jit(solution)/shard_map/all_gather | solution.py:114
  8.7 0.6 copy-start.13
  9.4 0.6 copy-start.9
  10.4 0.6 copy-start.18
  11.7 10.7 %copy-start.22 = (s32[40,8]{0,1:T(8,128)S(1)}, s32[40,8]{0,1:T(8,128)}, u32[]{:S(2)}) copy-start(s32[40,8]{0,1:T(8,128)} %param.19) | copy-start | bytes 3844
  13.7 10.4 %copy-start.5 = (bf16[40,1024]{1,0:T(8,128)(2,1)S(1)}, bf16[40,1024]{1,0:T(8,128)(2,1)}, u32[]{:S(2)}) copy-start(bf16[40,1024]{1,0:T(8,128)(2,1)} %param.17) | copy-start | bytes 245764
  13.7 10.4 %copy-start.19 = (s32[448]{0:T(512)S(1)}, s32[448]{0:T(512)}, u32[]{:S(2)}) copy-start(s32[448]{0:T(512)} %copy-done.18) | copy-start | bytes 5380
  13.7 28.1 %all-to-all-start = ((bf16[32,2,7,1024]{3,1,2,0:T(2,128)(2,1)}), bf16[32,2,7,1024]{3,1,2,0:T(2,128)(2,1)S(1)}, u32[]{:S(2)}, u32[]{:S(2)}) async-start(bf16[32,2,7,1024]{3,1,2,0:T(2,128)(2,1)} %copy.67), calls=%async_computation | async-start | bytes 1835008 | tf_op jit(solution)/shard_map/all_to_all | solution.py:81
  22.5 0.6 copy-start.15
  23.2 0.6 copy-start.11
  41.8 0.9 copy-start.2
  42.7 21.4 %all-to-all-start.1 = ((bf16[32,2,7,1024]{3,1,2,0:T(2,128)(2,1)}), bf16[32,2,7,1024]{3,1,2,0:T(2,128)(2,1)}, u32[]{:S(2)}, u32[]{:S(2)}) async-start(bf16[32,2,7,1024]{3,1,2,0:T(2,128)(2,1)} %copy.71), calls=%async_computation.1 | async-start | bytes 1835008 | tf_op jit(solution)/shard_map/all_to_all | solution.py:82
  64.1 1.7 copy-start.4
  75.2 5.8 %copy-start.23 = (f32[40,8]{0,1:T(8,128)S(1)}, f32[40,8]{0,1:T(8,128)}, u32[]{:S(2)}) copy-start(f32[40,8]{0,1:T(8,128)} %param.21) | copy-start | bytes 3844
  75.2 5.9 %copy-start.16 = (s32[40,8]{1,0:T(8,128)S(1)}, s32[40,8]{1,0:T(8,128)}, u32[]{:S(2)}) copy-start(s32[40,8]{1,0:T(8,128)} %copy-done.15) | copy-start | bytes 3844
  75.2 6.1 %copy-start.12 = (s32[40,64]{0,1:T(8,128)S(1)}, s32[40,64]{0,1:T(8,128)}, u32[]{:S(2)}) copy-start(s32[40,64]{0,1:T(8,128)} %copy-done.11) | copy-start | bytes 30724
  77.1 4.4 %copy-start.24 = (f32[40,8]{0,1:T(8,128)S(1)}, f32[40,8]{0,1:T(8,128)}, u32[]{:S(2)}) copy-start(f32[40,8]{0,1:T(8,128)} %param.20) | copy-start | bytes 3844
  77.1 4.4 %copy-start.14 = (s32[40,8]{1,0:T(8,128)S(1)}, s32[40,8]{1,0:T(8,128)}, u32[]{:S(2)}) copy-start(s32[40,8]{1,0:T(8,128)} %copy-done.13) | copy-start | bytes 3844
  77.1 27.7 %all-to-all-start.3 = ((bf16[32,2,7,1024]{3,1,2,0:T(2,128)(2,1)}), bf16[32,2,7,1024]{3,1,2,0:T(2,128)(2,1)S(1)}, u32[]{:S(2)}, u32[]{:S(2)}) async-start(bf16[32,2,7,1024]{3,1,2,0:T(2,128)(2,1)} %copy.78), calls=%async_computation.3 | async-start | bytes 1835008 | tf_op jit(solution)/shard_map/all_to_all | solution.py:92
  81.8 29.2 %copy-start.10 = (s32[40,64]{0,1:T(8,128)S(1)}, s32[40,64]{0,1:T(8,128)}, u32[]{:S(2)}) copy-start(s32[40,64]{0,1:T(8,128)} %copy-done.9) | copy-start | bytes 30724
  81.8 30.0 %copy-start.20 = (s32[256]{0:T(256)S(1)}, s32[256]{0:T(256)}, u32[]{:S(2)}) copy-start(s32[256]{0:T(256)} %param.28) | copy-start | bytes 3076
  81.8 30.4 %copy-start.28 = (u32[256]{0:T(256)S(1)}, u32[256]{0:T(256)}, u32[]{:S(2)}) copy-start(u32[256]{0:T(256)} %constant.68) | copy-start | bytes 3076
  81.8 31.6 %copy-start.27 = (s32[40]{0:T(128)S(1)}, s32[40]{0:T(128)}, u32[]{:S(2)}) copy-start(s32[40]{0:T(128)} %param.27) | copy-start | bytes 484
  104.8 32.7 %all-to-all-start.2 = ((bf16[32,2,7,1024]{3,1,2,0:T(2,128)(2,1)}), bf16[32,2,7,1024]{3,1,2,0:T(2,128)(2,1)S(1)}, u32[]{:S(2)}, u32[]{:S(2)}) async-start(bf16[32,2,7,1024]{3,1,2,0:T(2,128)(2,1)} %copy.74), calls=%async_computation.2 | async-start | bytes 1835008 | tf_op jit(solution)/shard_map/all_to_all | solution.py:91
  137.5 1.2 copy-start.3
  137.5 1.2 copy-start.6
  137.8 1.6 copy-start.8
  138.7 2.4 copy-start.21
  195.3 13.5 %copy-start.17 = (s32[9728]{0:T(1024)S(1)}, s32[9728]{0:T(1024)}, u32[]{:S(2)}) copy-start(s32[9728]{0:T(1024)} %iota_add_fusion) | copy-start | bytes 116740
  208.8 66.7 %copy-start.26 = (s32[256]{0:T(256)S(1)}, s32[256]{0:T(256)}, u32[]{:S(2)}) copy-start(s32[256]{0:T(256)} %get-tuple-element.67) | copy-start | bytes 3076
  208.8 66.7 %copy-start.29 = (s32[40]{0:T(128)S(1)}, s32[40]{0:T(128)}, u32[]{:S(2)}) copy-start(s32[40]{0:T(128)} %iota_add_fusion.1) | copy-start | bytes 484
  208.8 173.4 %copy-start.25 = (s32[256]{0:T(256)S(1)}, s32[256]{0:T(256)}, u32[]{:S(2)}) copy-start(s32[256]{0:T(256)} %param.29) | copy-start | bytes 3076
  208.8 174.0 %copy-start.1 = (bf16[2,384,1024]{2,1,0:T(8,128)(2,1)S(1)}, bf16[2,384,1024]{2,1,0:T(8,128)(2,1)}, u32[]{:S(2)}) copy-start(bf16[2,384,1024]{2,1,0:T(8,128)(2,1)} %param.24) | copy-start | bytes 4718596
Sparse Core Ops, SparseCore 0:
  10.6 105.0 all-gather.3
where the time goes:
time: 391 us; the launch traced here: 390 us
  blocking collectives  222 us (57%)
  waiting for transfers between devices  49.2 us (13%)
  matrix products  38.7 us (10%)
  local copies, waits for them, and re-layouts  24.4 us (6%)
  starting transfers between devices  24.2 us (6%)
  other arithmetic  16.1 us (4%)
  between operations  15.3 us (4%)
    psum x1, blocking collectives, local(): sums = lax.psum(partial_value, ('grp', 'ep'))  107 us
    all_gather x3, blocking collectives, joined_2(): pieces = jax.tree.map(lambda part: lax.all_gather(part, axis), value)  54 us
    dot_general x2, matrix products, vocab_stats(): jnp.einsum('td,vd->tv', row_block, weights, preferred_element_type=jnp.fl...  26.9 us
    all_to_all x1, waiting for transfers between devices, local(): lax.all_to_all(outputs[:, :, slots:], 'ep', split_axis=0, concat_axis=0,...  21.1 us
    all_gather x1, blocking collectives, local(): lax.all_gather(ref_normed, 'grp', axis=0, tiled=True)  20.5 us
    unnamed x1, blocking collectives  20.4 us
    all_gather x1, blocking collectives, local(): lax.all_gather(pol_normed, 'grp', axis=0, tiled=True)  20.2 us
    all_to_all x1, waiting for transfers between devices, local(): lax.all_to_all(ref_send, 'ep', split_axis=0, concat_axis=0, tiled=True)  14.5 us
  transfers between devices with their start and end apart: 5, of which 3 were waited for; matrix products, arithmetic and copies ran while one was open for 9% of the time, Pallas kernels for 0%

commit v1 on v0

--- a/solution.py
+++ b/solution.py
@@ -133,7 +133,7 @@
     partial_value = jnp.dot(
         token_ratio, inside.astype(jnp.float32), precision=lax.Precision.HIGHEST
     ) / seq_lengths.astype(jnp.float32)
-    sums = lax.psum(partial_value, ("grp", "ep"))
+    sums = lax.psum(lax.psum(partial_value, "ep"), "grp")
     owned = jnp.sum(jnp.where(owners == device_index, sums, 0.0)).reshape(1)
     return (token_ratio, owned)
 

time: 391 us -> 392 us (level)
    psum x1 -> x2, blocking collectives: 107 us -> 107 us  [local(): sums = lax.psum(lax.psum(partial_value, 'ep'), 'grp')]
where the time goes in v1:
time: 392 us; the launch traced here: 390 us
  blocking collectives  222 us (57%)
  waiting for transfers between devices  49.2 us (13%)
  matrix products  38.7 us (10%)
  local copies, waits for them, and re-layouts  24.4 us (6%)
  starting transfers between devices  24.2 us (6%)
  other arithmetic  16.1 us (4%)
  between operations  15.3 us (4%)
    psum x2, blocking collectives, local(): sums = lax.psum(lax.psum(partial_value, 'ep'), 'grp')  107 us
    all_gather x3, blocking collectives, joined_2(): pieces = jax.tree.map(lambda part: lax.all_gather(part, axis), value)  54 us
    dot_general x2, matrix products, vocab_stats(): jnp.einsum('td,vd->tv', row_block, weights, preferred_element_type=jnp.fl...  26.9 us
    all_to_all x1, waiting for transfers between devices, local(): lax.all_to_all(outputs[:, :, slots:], 'ep', split_axis=0, concat_axis=0,...  21.1 us
    all_gather x1, blocking collectives, local(): lax.all_gather(ref_normed, 'grp', axis=0, tiled=True)  20.5 us
    unnamed x1, blocking collectives  20.4 us
    all_gather x1, blocking collectives, local(): lax.all_gather(pol_normed, 'grp', axis=0, tiled=True)  20.2 us
    all_to_all x1, waiting for transfers between devices, local(): lax.all_to_all(ref_send, 'ep', split_axis=0, concat_axis=0, tiled=True)  14.5 us
  transfers between devices with their start and end apart: 5, of which 3 were waited for; matrix products, arithmetic and copies ran while one was open for 9% of the time, Pallas kernels for 0%

profile of v1, /device:TPU:1, one launch (start us, length us, event | category | flops | bytes accessed | tf_op | source)
XLA Modules:
  0.0 390.0 jit_solution(1898214476692453274)
XLA Ops:
  7.2 0.7 all-gather.4.cloned.1.call-update
  7.9 0.8 copy.62
  9.4 0.6 copy-done.9
  10.4 0.6 copy-done.18
  11.0 0.4 convolution_convert_fusion.1
  11.8 2.0 copy.67
  13.7 8.7 %all-to-all-start = ((bf16[32,2,7,1024]{3,1,2,0:T(2,128)(2,1)}), bf16[32,2,7,1024]{3,1,2,0:T(2,128)(2,1)S(1)}, u32[]{:S(2)}, u32[]{:S(2)}) async-start(bf16[32,2,7,1024]{3,1,2,0:T(2,128)(2,1)} %copy.67), calls=%async_computation | async-start | bytes 1835008 | tf_op jit(solution)/shard_map/all_to_all | solution.py:81
  22.7 0.4 copy-done.15
  23.2 0.6 copy-done.11
  24.1 1.4 convolution_convert_fusion
  25.5 1.4 reshape.318
  27.0 2.0 copy.71
  28.9 12.9 %all-to-all-done = bf16[32,2,7,1024]{3,1,2,0:T(2,128)(2,1)S(1)} async-done(((bf16[32,2,7,1024]{3,1,2,0:T(2,128)(2,1)}), bf16[32,2,7,1024]{3,1,2,0:T(2,128)(2,1)S(1)}, u32[]{:S(2)}, u32[]{:S(2)}) %all-to-all-start) | async-done | bytes 917536 | tf_op jit(solution)/shard_map/all_to_all | solution.py:81
  41.8 0.9 copy-done.2
  42.7 5.4 %all-to-all-start.1 = ((bf16[32,2,7,1024]{3,1,2,0:T(2,128)(2,1)}), bf16[32,2,7,1024]{3,1,2,0:T(2,128)(2,1)}, u32[]{:S(2)}, u32[]{:S(2)}) async-start(bf16[32,2,7,1024]{3,1,2,0:T(2,128)(2,1)} %copy.71), calls=%async_computation.1 | async-start | bytes 1835008 | tf_op jit(solution)/shard_map/all_to_all | solution.py:82
  48.2 1.4 copy_dynamic-update-slice_fusion.1
  49.6 14.5 %all-to-all-done.1 = bf16[32,2,7,1024]{3,1,2,0:T(2,128)(2,1)} async-done(((bf16[32,2,7,1024]{3,1,2,0:T(2,128)(2,1)}), bf16[32,2,7,1024]{3,1,2,0:T(2,128)(2,1)}, u32[]{:S(2)}, u32[]{:S(2)}) %all-to-all-start.1) | async-done | bytes 917536 | tf_op jit(solution)/shard_map/all_to_all | solution.py:82
  64.1 1.5 copy_dynamic-update-slice_fusion
  65.8 2.2 fusion.9
  68.0 5.2 %convert_bitcast_fusion = bf16[32,2,14,1024]{3,0,2,1:T(8,128)(2,1)} fusion(bf16[2,384,1024]{2,1,0:T(8,128)(2,1)S(1)} %copy-done, bf16[32,2,14,1024]{3,0,2,1:T(8,128)(2,1)S(1)} %copy_dynamic-update-slice_fusion, bf16[2,1024,384]{2,1,0:T(8,128)(2,1)} %param.23, f32[32,2,14,384]{3,0,2,1:T(8,128)} %fusion.9), kind=kOutput, calls=%fused_computation.12 | convolution fusion | flops 1412268032 | bytes 8192000 | tf_op jit(solution)/shard_map/nesf,efd->nesd/dot_general | solution.py:88
  73.2 1.9 fusion.44
  75.2 1.9 copy.78
  77.1 3.9 all-to-all-start.3
  81.8 1.9 copy.74
  83.7 21.1 %all-to-all-done.3 = bf16[32,2,7,1024]{3,1,2,0:T(2,128)(2,1)S(1)} async-done(((bf16[32,2,7,1024]{3,1,2,0:T(2,128)(2,1)}), bf16[32,2,7,1024]{3,1,2,0:T(2,128)(2,1)S(1)}, u32[]{:S(2)}, u32[]{:S(2)}) %all-to-all-start.3) | async-done | bytes 917536 | tf_op jit(solution)/shard_map/all_to_all | solution.py:92
  104.8 6.1 %all-to-all-start.2 = ((bf16[32,2,7,1024]{3,1,2,0:T(2,128)(2,1)}), bf16[32,2,7,1024]{3,1,2,0:T(2,128)(2,1)S(1)}, u32[]{:S(2)}, u32[]{:S(2)}) async-start(bf16[32,2,7,1024]{3,1,2,0:T(2,128)(2,1)} %copy.74), calls=%async_computation.2 | async-start | bytes 1835008 | tf_op jit(solution)/shard_map/all_to_all | solution.py:91
  111.0 0.7 mul.94
  112.2 0.6 dynamic-slice
  113.7 20.4 %all-reduce = s32[320]{0:T(512)S(1)} all-reduce(s32[320]{0:T(512)S(1)} %dynamic-update-slice), channel_id=1, replica_groups=mesh['grp'=8,'ep'=32] {'grp'}, use_global_device_ids=true, to_apply=%add | all-reduce | flops 320 | bytes 2560
  134.0 0.6 iota_add_fusion.1
  134.7 0.6 fusion.43
  135.4 0.6 iota_add_fusion
  136.3 1.2 reshape.320
  138.1 0.6 copy-done.3
  138.7 0.7 multiply_reduce_fusion
  139.4 1.7 multiply_reduce_fusion.1
  141.2 20.2 %all_gather.26 = bf16[320,1024]{1,0:T(8,128)(2,1)S(1)} all-gather(bf16[40,1024]{1,0:T(8,128)(2,1)S(1)} %get-tuple-element.71), channel_id=1, replica_groups=mesh['grp'=8,'ep'=32] {'grp'}, dimensions={0}, use_global_device_ids=true | all-gather | bytes 737280 | tf_op jit(solution)/shard_map/all_gather | solution.py:107
  161.4 20.5 %all_gather.28 = bf16[320,1024]{1,0:T(8,128)(2,1)S(1)} all-gather(bf16[40,1024]{1,0:T(8,128)(2,1)S(1)} %get-tuple-element.72), channel_id=1, replica_groups=mesh['grp'=8,'ep'=32] {'grp'}, dimensions={0}, use_global_device_ids=true | all-gather | bytes 737280 | tf_op jit(solution)/shard_map/all_gather | solution.py:108
  181.9 13.4 %fusion.45 = (f32[320]{0:T(512)S(1)}, f32[320,9728]{1,0:T(8,128)}) fusion(bf16[320,1024]{1,0:T(8,128)(2,1)S(1)} %all_gather.26, bf16[9728,1024]{1,0:T(8,128)(2,1)} %all-gather.4.cloned.1.call-done), kind=kOutput, calls=%fused_computation.84 | convolution fusion | flops 6378454528 | bytes 33031424 | tf_op jit(solution)/shard_map/td,vd->tv/dot_general | solution.py:24
  195.3 13.5 %fusion.46 = (f32[320]{0:T(512)S(1)}, f32[320,9728]{1,0:T(8,128)}) fusion(bf16[320,1024]{1,0:T(8,128)(2,1)S(1)} %all_gather.28, bf16[9728,1024]{1,0:T(8,128)(2,1)} %all-gather.4.cloned.1.call-done), kind=kOutput, calls=%fused_computation.85 | convolution fusion | flops 6378454528 | bytes 33031424 | tf_op jit(solution)/shard_map/td,vd->tv/dot_general | solution.py:24
  208.8 11.5 %fusion.2 = (f32[320]{0:T(512)S(1)}, f32[320]{0:T(512)S(1)}, f32[320]{0:T(512)S(1)}, f32[320]{0:T(512)S(1)}) fusion(f32[320,9728]{1,0:T(8,128)} %get-tuple-element.80, s32[9728]{0:T(1024)S(1)} %copy-done.17, s32[320]{0:T(512)S(1)} %all-reduce, f32[320]{0:T(512)S(1)} %get-tuple-element.79, f32[320,9728]{1,0:T(8,128)} %get-tuple-element.82, ...), kind=kLoop, calls=%fused_computation.8 | loop fusion | flops 28015360 | bytes 24951552 | tf_op jit(solution)/shard_map/reduce_sum | solution.py:27
  220.3 18.0 %all-gather.1 = f32[8,2,320]{2,1,0:T(2,128)S(1)} all-gather(f32[1,2,320]{2,1,0:T(2,128)S(1)} %maximum_bitcast_fusion), channel_id=2, replica_groups=mesh['grp'=8,'ep'=32] {'grp'}, dimensions={0}, use_global_device_ids=true | all-gather | bytes 23040 | tf_op jit(solution)/shard_map/all_gather | solution.py:8
  238.4 18.0 %all_gather.30 = f32[8,2,320]{2,1,0:T(2,128)S(1)} all-gather(f32[1,2,320]{2,1,0:T(2,128)S(1)} %get-tuple-element.73), channel_id=1, replica_groups=mesh['grp'=8,'ep'=32] {'grp'}, dimensions={0}, use_global_device_ids=true | all-gather | bytes 23040 | tf_op jit(solution)/shard_map/all_gather | solution.py:8
  256.5 18.0 %all_gather.29 = f32[8,2,320]{2,1,0:T(2,128)S(1)} all-gather(f32[1,2,320]{2,1,0:T(2,128)S(1)} %get-tuple-element.74), channel_id=1, replica_groups=mesh['grp'=8,'ep'=32] {'grp'}, dimensions={0}, use_global_device_ids=true | all-gather | bytes 23040 | tf_op jit(solution)/shard_map/all_gather | solution.py:8
  274.9 0.5 fusion.42
  275.7 94.9 %psum.14 = f32[256]{0:T(256)S(1)} all-reduce(f32[256]{0:T(256)S(1)} %convert_divide_fusion), channel_id=1, replica_groups=mesh['grp'=8,'ep'=32] {'ep'}, use_global_device_ids=true, to_apply=%region_18.19 | all-reduce | flops 256 | bytes 2048 | tf_op jit(solution)/shard_map/psum | solution.py:136
  370.5 12.0 %psum.15 = f32[256]{0:T(256)S(1)} all-reduce(f32[256]{0:T(256)S(1)} %psum.14), channel_id=1, replica_groups=mesh['grp'=8,'ep'=32] {'grp'}, use_global_device_ids=true, to_apply=%region_19.20 | all-reduce | flops 256 | bytes 2048 | tf_op jit(solution)/shard_map/psum | solution.py:136
  382.6 0.6 fusion.39
  (126 shorter events, 5.7 us)
Async XLA Ops:
  7.2 60.8 %copy-start = (bf16[2,384,1024]{2,1,0:T(8,128)(2,1)S(1)}, bf16[2,384,1024]{2,1,0:T(8,128)(2,1)}, u32[]{:S(2)}) copy-start(bf16[2,384,1024]{2,1,0:T(8,128)(2,1)} %param.24) | copy-start | bytes 4718596
  7.2 3.8 copy-start.7
  7.2 174.7 %all-gather.4.cloned.1.call-start = ((), (), s32[]{:S(2)}) async-start(), calls=%async_computation.4 | async-start | bytes 20545536 | tf_op jit(solution)/shard_map/all_gather | solution.py:114
  8.7 0.6 copy-start.13
  9.4 0.6 copy-start.9
  10.4 0.6 copy-start.18
  11.7 10.7 %copy-start.22 = (s32[40,8]{0,1:T(8,128)S(1)}, s32[40,8]{0,1:T(8,128)}, u32[]{:S(2)}) copy-start(s32[40,8]{0,1:T(8,128)} %param.19) | copy-start | bytes 3844
  13.7 10.4 %copy-start.5 = (bf16[40,1024]{1,0:T(8,128)(2,1)S(1)}, bf16[40,1024]{1,0:T(8,128)(2,1)}, u32[]{:S(2)}) copy-start(bf16[40,1024]{1,0:T(8,128)(2,1)} %param.17) | copy-start | bytes 245764
  13.7 10.4 %copy-start.19 = (s32[448]{0:T(512)S(1)}, s32[448]{0:T(512)}, u32[]{:S(2)}) copy-start(s32[448]{0:T(512)} %copy-done.18) | copy-start | bytes 5380
  13.7 28.1 %all-to-all-start = ((bf16[32,2,7,1024]{3,1,2,0:T(2,128)(2,1)}), bf16[32,2,7,1024]{3,1,2,0:T(2,128)(2,1)S(1)}, u32[]{:S(2)}, u32[]{:S(2)}) async-start(bf16[32,2,7,1024]{3,1,2,0:T(2,128)(2,1)} %copy.67), calls=%async_computation | async-start | bytes 1835008 | tf_op jit(solution)/shard_map/all_to_all | solution.py:81
  22.5 0.6 copy-start.15
  23.2 0.6 copy-start.11
  41.8 0.9 copy-start.2
  42.7 21.4 %all-to-all-start.1 = ((bf16[32,2,7,1024]{3,1,2,0:T(2,128)(2,1)}), bf16[32,2,7,1024]{3,1,2,0:T(2,128)(2,1)}, u32[]{:S(2)}, u32[]{:S(2)}) async-start(bf16[32,2,7,1024]{3,1,2,0:T(2,128)(2,1)} %copy.71), calls=%async_computation.1 | async-start | bytes 1835008 | tf_op jit(solution)/shard_map/all_to_all | solution.py:82
  64.1 1.7 copy-start.4
  75.2 5.8 %copy-start.23 = (f32[40,8]{0,1:T(8,128)S(1)}, f32[40,8]{0,1:T(8,128)}, u32[]{:S(2)}) copy-start(f32[40,8]{0,1:T(8,128)} %param.21) | copy-start | bytes 3844
  75.2 5.9 %copy-start.16 = (s32[40,8]{1,0:T(8,128)S(1)}, s32[40,8]{1,0:T(8,128)}, u32[]{:S(2)}) copy-start(s32[40,8]{1,0:T(8,128)} %copy-done.15) | copy-start | bytes 3844
  75.2 6.1 %copy-start.12 = (s32[40,64]{0,1:T(8,128)S(1)}, s32[40,64]{0,1:T(8,128)}, u32[]{:S(2)}) copy-start(s32[40,64]{0,1:T(8,128)} %copy-done.11) | copy-start | bytes 30724
  77.1 4.4 %copy-start.24 = (f32[40,8]{0,1:T(8,128)S(1)}, f32[40,8]{0,1:T(8,128)}, u32[]{:S(2)}) copy-start(f32[40,8]{0,1:T(8,128)} %param.20) | copy-start | bytes 3844
  77.1 4.4 %copy-start.14 = (s32[40,8]{1,0:T(8,128)S(1)}, s32[40,8]{1,0:T(8,128)}, u32[]{:S(2)}) copy-start(s32[40,8]{1,0:T(8,128)} %copy-done.13) | copy-start | bytes 3844
  77.1 27.7 %all-to-all-start.3 = ((bf16[32,2,7,1024]{3,1,2,0:T(2,128)(2,1)}), bf16[32,2,7,1024]{3,1,2,0:T(2,128)(2,1)S(1)}, u32[]{:S(2)}, u32[]{:S(2)}) async-start(bf16[32,2,7,1024]{3,1,2,0:T(2,128)(2,1)} %copy.78), calls=%async_computation.3 | async-start | bytes 1835008 | tf_op jit(solution)/shard_map/all_to_all | solution.py:92
  81.8 29.2 %copy-start.10 = (s32[40,64]{0,1:T(8,128)S(1)}, s32[40,64]{0,1:T(8,128)}, u32[]{:S(2)}) copy-start(s32[40,64]{0,1:T(8,128)} %copy-done.9) | copy-start | bytes 30724
  81.8 30.0 %copy-start.20 = (s32[256]{0:T(256)S(1)}, s32[256]{0:T(256)}, u32[]{:S(2)}) copy-start(s32[256]{0:T(256)} %param.28) | copy-start | bytes 3076
  81.8 30.4 %copy-start.28 = (u32[256]{0:T(256)S(1)}, u32[256]{0:T(256)}, u32[]{:S(2)}) copy-start(u32[256]{0:T(256)} %constant.68) | copy-start | bytes 3076
  81.8 31.6 %copy-start.27 = (s32[40]{0:T(128)S(1)}, s32[40]{0:T(128)}, u32[]{:S(2)}) copy-start(s32[40]{0:T(128)} %param.27) | copy-start | bytes 484
  104.8 32.7 %all-to-all-start.2 = ((bf16[32,2,7,1024]{3,1,2,0:T(2,128)(2,1)}), bf16[32,2,7,1024]{3,1,2,0:T(2,128)(2,1)S(1)}, u32[]{:S(2)}, u32[]{:S(2)}) async-start(bf16[32,2,7,1024]{3,1,2,0:T(2,128)(2,1)} %copy.74), calls=%async_computation.2 | async-start | bytes 1835008 | tf_op jit(solution)/shard_map/all_to_all | solution.py:91
  137.5 1.2 copy-start.3
  137.5 1.2 copy-start.6
  137.8 1.6 copy-start.8
  138.7 2.4 copy-start.21
  195.3 13.5 %copy-start.17 = (s32[9728]{0:T(1024)S(1)}, s32[9728]{0:T(1024)}, u32[]{:S(2)}) copy-start(s32[9728]{0:T(1024)} %iota_add_fusion) | copy-start | bytes 116740
  208.8 66.7 %copy-start.26 = (s32[256]{0:T(256)S(1)}, s32[256]{0:T(256)}, u32[]{:S(2)}) copy-start(s32[256]{0:T(256)} %get-tuple-element.67) | copy-start | bytes 3076
  208.8 66.7 %copy-start.29 = (s32[40]{0:T(128)S(1)}, s32[40]{0:T(128)}, u32[]{:S(2)}) copy-start(s32[40]{0:T(128)} %iota_add_fusion.1) | copy-start | bytes 484
  208.8 173.7 %copy-start.25 = (s32[256]{0:T(256)S(1)}, s32[256]{0:T(256)}, u32[]{:S(2)}) copy-start(s32[256]{0:T(256)} %param.29) | copy-start | bytes 3076
  208.8 174.3 %copy-start.1 = (bf16[2,384,1024]{2,1,0:T(8,128)(2,1)S(1)}, bf16[2,384,1024]{2,1,0:T(8,128)(2,1)}, u32[]{:S(2)}) copy-start(bf16[2,384,1024]{2,1,0:T(8,128)(2,1)} %param.24) | copy-start | bytes 4718596
Sparse Core Ops, SparseCore 0:
  10.6 105.0 all-gather.3
